TPU v7x, 32 devices: a whole 2x2x4 slice. The times are simulated.
32 devices in a mesh: arc: 8 (over y, x, core), par: 4 (over z).
Axes of the slice: x: 2, y: 2, z: 4, core: 2. Of those that a mesh axis runs over, the one named last changes fastest.
Arguments:
- partials: bfloat16 [8, 3, 128, 8192], P('arc', None, 'par'), may hold values from -6 to 6
- epoch_index: int32 [8, 128], P('arc'), may hold values from 0 to 511, as said below
- whitening: float32 [8, 3, 128, 128], P('arc'), may hold values from -2 to 2, as said below
Outputs:
- normal_matrix: float32 [8192, 8192], P('arc', 'par')
Inputs may be any that keep to these rules, and one draw needn't show every extreme that they name: `epoch_index`: in each arc the epoch indices rise strictly; the first is 0 and the last is 511. `whitening`: each block is lower triangular with diagonal entries between 1 and 2.
All inputs are finite; a program needn't handle non-finite values.
Results may differ from a plain program's by a relative error of at most 0.0003.
Values may be sent and summed in bfloat16 or wider, within the bound.
No kernel may reach another device: no remote copies, remote signals or barrier semaphores. Data moves between devices by JAX's collectives and lax.ppermute only.
A program may use at most 128 MiB of HBM per device.

v0:
```python
import math
import jax
import jax.numpy as jnp
from jax import lax
from jax.sharding import PartitionSpec as P

KERNEL_GAIN = 8.0


def from_root(block, axis, owner):
    block = jnp.where(lax.axis_index(axis) == owner, block, jnp.zeros_like(block))
    return lax.psum(block, axis)


def mixing_matrices(epoch_index, whitening, epochs, row_scale):
    times_arc = epoch_index.astype(jnp.float32) / jnp.float32(4 * epochs - 1)
    later_time = times_arc[:, :, None]
    earlier_time = times_arc[:, None, :]
    green_part = jnp.minimum(later_time, earlier_time) * (
        1.0 - jnp.maximum(later_time, earlier_time)
    )
    kernel = jnp.eye(epochs, dtype=jnp.float32)[None] + KERNEL_GAIN / epochs * green_part
    mixing = jnp.einsum("acij,ajk->acik", whitening, kernel, precision=lax.Precision.HIGHEST)
    return mixing * row_scale


def on_device(partials, epoch_index, whitening):
    arc_local = partials.shape[0]
    epochs = epoch_index.shape[1]
    param_count = partials.shape[3]
    arc_count = lax.axis_size("arc")
    par_count = lax.axis_size("par")
    total_arcs = arc_local * arc_count
    col_block = param_count // par_count
    row_block = param_count // arc_count
    row_scale = 1.0 / math.sqrt(3 * epochs * total_arcs)
    mixing = mixing_matrices(epoch_index, whitening, epochs, row_scale)
    columns = lax.all_to_all(partials, "par", split_axis=3, concat_axis=2, tiled=True)
    arc_position = lax.axis_index("arc")
    holder = arc_position * row_block // col_block
    offset = arc_position * row_block - holder * col_block
    raw_cols = lax.all_gather(columns, "arc", axis=0, tiled=True)
    all_mixing = lax.all_gather(mixing, "arc", axis=0, tiled=True)
    gathered = jnp.einsum(
        "acij,acjk->acik", all_mixing, raw_cols.astype(jnp.float32), precision=lax.Precision.HIGHEST
    )
    raw_piece = lax.dynamic_slice_in_dim(raw_cols, offset, row_block, 3)
    raw_rows = from_root(raw_piece, "par", holder)
    row_data = jnp.einsum(
        "acij,acjk->acik", all_mixing, raw_rows.astype(jnp.float32), precision=lax.Precision.HIGHEST
    )
    row_flat = row_data.reshape(-1, row_block)
    col_flat = gathered.reshape(-1, col_block)
    return lax.dot_general(
        row_flat,
        col_flat,
        (((0,), (0,)), ((), ())),
        precision=lax.Precision.HIGHEST,
        preferred_element_type=jnp.float32,
    )


def solution(mesh):
    placed = (P("arc", None, "par", None), P("arc", None), P("arc", None, None, None))
    return jax.shard_map(
        on_device, mesh=mesh, in_specs=placed, out_specs=P("arc", "par"), check_vma=False
    )
```

profile of v0, /device:TPU:0, one launch (start us, length us, event | category | flops | bytes accessed | tf_op | source)
XLA Modules:
  0.0 509.8 jit_solution(11392306326867929905)
XLA Ops:
  6.5 0.0 copy-start
  6.5 0.0 all-gather.4.cloned.1.call-start
  6.5 10.6 %copy.9 = bf16[1,3,32,8192]{2,1,0,3:T(4,128)(2,1)} copy(bf16[1,3,32,8192]{3,2,1,0:T(8,128)(2,1)} %param.3) | data formatting | bytes 3145728 | tf_op args[0]
  17.2 7.4 %reshape.216 = bf16[4,2,98304]{2,1,0:T(2,128)(2,1)S(1)} reshape(bf16[8192,1,3,32]{3,2,1,0:T(4,128)(2,1)} %bitcast.29) | data formatting | bytes 3145728
  24.6 43.1 %all_to_all.18 = bf16[4,2,98304]{2,1,0:T(2,128)(2,1)S(1)} all-to-all(bf16[4,2,98304]{2,1,0:T(2,128)(2,1)S(1)} %reshape.216), channel_id=1, replica_groups=mesh['arc'=8,'par'=4] {'par'}, dimensions={0} | all-to-all | bytes 3145728 | tf_op jit(solution)/shard_map/all_to_all | solution.py:38
  67.7 7.0 %reshape.217 = bf16[8192,1,3,32]{3,2,1,0:T(4,128)(2,1)} reshape(bf16[4,2,98304]{2,1,0:T(2,128)(2,1)S(1)} %all_to_all.18) | data formatting | bytes 3145728
  74.8 0.0 copy-start.3
  74.8 11.6 %copy.15 = bf16[1,3,32,4,2048]{4,3,2,1,0:T(4,128)(2,1)S(1)} copy(bf16[1,3,32,4,2048]{2,1,4,3,0:T(4,128)(2,1)} %bitcast.28) | data formatting | bytes 3145728 | tf_op jit(solution)/shard_map/all_to_all | solution.py:38
  86.4 2.0 copy.11
  88.4 0.0 all-gather.4.cloned.1.call-update
  88.4 0.0 all-gather.6.cloned.1.call-start
  88.4 0.0 copy-done.3
  88.5 0.0 copy-done
  88.5 0.4 fusion
  88.9 0.8 copy.8
  89.7 0.0 all-gather.6.cloned.1.call-update
  89.7 0.2 all-reduce.2.cloned.1.call-start
  90.0 69.7 %all-gather.4.cloned.1.call-done = bf16[8,3,128,2048]{3,2,1,0:T(8,128)(2,1)} async-done(((bf16[1,3,128,2048]{3,2,1,0:T(8,128)(2,1)}), bf16[8,3,128,2048]{3,2,1,0:T(8,128)(2,1)}) %all-gather.4.cloned.1.call-update) | async-done | bytes 12582928 | tf_op jit(solution)/shard_map/all_gather | solution.py:42
  159.7 7.5 %dynamic-slice_select_fusion = bf16[8,3,128,1024]{3,2,1,0:T(8,128)(2,1)} fusion(bf16[8,3,128,2048]{3,2,1,0:T(8,128)(2,1)} %all-gather.4.cloned.1.call-done, s32[]{:T(128)S(6)} %select_n.18, pred[]{:T(512)S(6)} %eq.22), kind=kLoop, calls=%fused_computation | loop fusion | flops 3145728 | bytes 12582917 | tf_op jit(solution)/shard_map/jit(_where)/select_n | solution.py:11
  167.2 0.0 all-reduce.2.cloned.1.call-update
  167.2 19.9 %all-gather.6.cloned.1.call-done = f32[24,128,128]{2,1,0:T(8,128)} async-done(((f32[3,128,128]{2,1,0:T(8,128)}), f32[24,128,128]{2,1,0:T(8,128)}) %all-gather.6.cloned.1.call-update) | async-done | bytes 1572880 | tf_op jit(solution)/shard_map/all_gather | solution.py:43
  187.2 0.0 copy-start.2
  187.2 18.1 %fusion.17 = f32[8,3,128,2048]{3,2,1,0:T(8,128)} fusion(f32[8,3,128,128]{3,2,1,0:T(8,128)} %bitcast.30, bf16[8,3,128,2048]{3,2,1,0:T(8,128)(2,1)} %all-gather.4.cloned.1.call-done), kind=kOutput, calls=%fused_computation.22 | convolution fusion | flops 9663676416 | bytes 39321600 | tf_op jit(solution)/shard_map/acij,acjk->acik/dot_general | solution.py:44
  205.3 207.1 %all-reduce.2.cloned.1.call-done = bf16[8,3,128,1024]{3,2,1,0:T(8,128)(2,1)} async-done(((bf16[8,3,128,1024]{3,2,1,0:T(8,128)(2,1)}), bf16[8,3,128,1024]{3,2,1,0:T(8,128)(2,1)}) %all-reduce.2.cloned.1.call-update) | async-done | bytes 6291472 | tf_op jit(solution)/shard_map/psum | solution.py:12
  412.4 0.0 copy-done.2
  412.4 8.3 %fusion.16 = f32[8,3,128,1024]{2,3,1,0:T(8,128)S(1)} fusion(f32[8,3,128,128]{3,2,1,0:T(8,128)S(1)} %bitcast.31, bf16[8,3,128,1024]{3,2,1,0:T(8,128)(2,1)} %all-reduce.2.cloned.1.call-done), kind=kOutput, calls=%fused_computation.21 | convolution fusion | flops 4831838208 | bytes 20447232 | tf_op jit(solution)/shard_map/acij,acjk->acik/dot_general | solution.py:49
  420.8 0.0 copy-start.1
  420.8 82.4 %convolution_bitcast_fusion = f32[1024,2048]{1,0:T(8,128)} fusion(f32[8,3,128,1024]{2,3,1,0:T(8,128)S(1)} %fusion.16, f32[8,3,128,2048]{3,2,1,0:T(8,128)} %fusion.17), kind=kOutput, calls=%fused_computation.1 | convolution fusion | flops 77309411328 | bytes 46137344 | tf_op jit(solution)/shard_map/dot_general | solution.py:54
  503.2 0.0 copy-done.1
  (1 shorter events, 0.0 us)
Async XLA Ops:
  6.5 81.9 %copy-start = (f32[1,3,128,128]{3,2,1,0:T(8,128)S(1)}, f32[1,3,128,128]{3,2,1,0:T(8,128)}, u32[]{:S(2)}) copy-start(f32[1,3,128,128]{3,2,1,0:T(8,128)} %param.5) | copy-start | bytes 589828
  6.5 153.2 %all-gather.4.cloned.1.call-start = ((), (), s32[]{:S(2)}) async-start(), calls=%async_computation.1 | async-start | bytes 14155776 | tf_op jit(solution)/shard_map/all_gather | solution.py:42
  74.8 13.7 %copy-start.3 = (s32[1,128]{1,0:T(1,128)S(1)}, s32[1,128]{1,0:T(1,128)}, u32[]{:S(2)}) copy-start(s32[1,128]{1,0:T(1,128)} %param.4) | copy-start | bytes 1540
  88.4 98.8 %all-gather.6.cloned.1.call-start = ((), (), s32[]{:S(2)}) async-start(), calls=%async_computation.3 | async-start | bytes 1769472 | tf_op jit(solution)/shard_map/all_gather | solution.py:43
  89.7 322.7 %all-reduce.2.cloned.1.call-start = ((), (), s32[]{:S(2)}) async-start(), calls=%async_computation.2 | async-start | bytes 12582912 | tf_op jit(solution)/shard_map/psum | solution.py:12
  187.2 225.3 %copy-start.2 = (f32[24,128,128]{2,1,0:T(8,128)S(1)}, f32[24,128,128]{2,1,0:T(8,128)}, u32[]{:S(2)}) copy-start(f32[24,128,128]{2,1,0:T(8,128)} %all-gather.6.cloned.1.call-done) | copy-start | bytes 4718596
  420.8 82.4 %copy-start.1 = (f32[1,3,128,128]{3,2,1,0:T(8,128)S(1)}, f32[1,3,128,128]{3,2,1,0:T(8,128)}, u32[]{:S(2)}) copy-start(f32[1,3,128,128]{3,2,1,0:T(8,128)} %param.5) | copy-start | bytes 589828
Sparse Core Ops, SparseCore 0:
  88.5 71.1 all-gather.3
  161.6 25.5 all-gather.5
  189.5 222.8 all-reduce.1
where the time goes:
time: 511 us; the launch traced here: 510 us
  waiting for transfers between devices  297 us (58%)
  matrix products  109 us (21%)
  blocking collectives  43.1 us (8%)
  local copies, waits for them, and re-layouts  39.5 us (8%)
  between operations  13.2 us (3%)
  other arithmetic  7.54 us (1%)
    psum x1, waiting for transfers between devices, from_root(): return lax.psum(block, axis)  207 us
    dot_general x1, matrix products, on_device(): lax.dot_general(row_flat, col_flat, (((0,), (0,)), ((), ())), precision=l...  82.4 us
    all_gather x1, waiting for transfers between devices, on_device(): raw_cols = lax.all_gather(columns, 'arc', axis=0, tiled=True)  69.7 us
    all_to_all x1, blocking collectives, on_device(): lax.all_to_all(partials, 'par', split_axis=3, concat_axis=2, tiled=True)  43.1 us
    unnamed x11, local copies, waits for them, and re-layouts  25.1 us
    all_gather x1, waiting for transfers between devices, on_device(): all_mixing = lax.all_gather(mixing, 'arc', axis=0, tiled=True)  19.9 us
    dot_general x1, matrix products, on_device(): jnp.einsum('acij,acjk->acik', all_mixing, raw_cols.astype(jnp.float32), p...  18.1 us
    all_to_all x2, local copies, waits for them, and re-layouts, on_device(): lax.all_to_all(partials, 'par', split_axis=3, concat_axis=2, tiled=True)  13.6 us
  transfers between devices with their start and end apart: 3, of which 3 were waited for; matrix products, arithmetic and copies ran while one was open for 5% of the time, Pallas kernels for 0%

commit v1 on v0

--- a/solution.py
+++ b/solution.py
@@ -1,3 +1,4 @@
+import functools
 import math
 import jax
 import jax.numpy as jnp
@@ -5,6 +6,18 @@
 from jax.sharding import PartitionSpec as P
 
 KERNEL_GAIN = 8.0
+
+
+def measure_bands(page, where_dim, dim_at):
+    return jnp.concatenate(
+        lax.all_to_all(
+            jnp.stack(jnp.split(page, lax.psum(1, "par"), axis=where_dim), 0), "par", 0, 0
+        ),
+        dim_at,
+    )
+
+
+tables_replace = functools.partial(measure_bands, where_dim=3, dim_at=2)
 
 
 def from_root(block, axis, owner):
@@ -35,7 +48,7 @@
     row_block = param_count // arc_count
     row_scale = 1.0 / math.sqrt(3 * epochs * total_arcs)
     mixing = mixing_matrices(epoch_index, whitening, epochs, row_scale)
-    columns = lax.all_to_all(partials, "par", split_axis=3, concat_axis=2, tiled=True)
+    columns = tables_replace(partials)
     arc_position = lax.axis_index("arc")
     holder = arc_position * row_block // col_block
     offset = arc_position * row_block - holder * col_block

time: 511 us -> 474 us (0.928)
  local copies, waits for them, and re-layouts: 39.5 us -> 3.57 us
    unnamed x11 -> x8, local copies, waits for them, and re-layouts: 25.1 us -> 0.02 us
    all_to_all x2 -> x1, local copies, waits for them, and re-layouts: 13.6 us -> 1.24 us  [measure_bands(): lax.all_to_all(jnp.stack(jnp.split(page, lax.psum(1, 'par'), axis=where_d...]
  transfers between devices with their start and end apart: 3 -> 3, of which waited for: 3 -> 3; matrix products, arithmetic and copies ran while one was open for 5% -> 6% of each run, Pallas kernels for 0% -> 0%
where the time goes in v1:
time: 474 us
  waiting for transfers between devices  297 us (63%)
  matrix products  109 us (23%)
  blocking collectives  43.1 us (9%)
  between operations  13.2 us (3%)
  other arithmetic  7.74 us (2%)
    psum x1, waiting for transfers between devices, from_root(): return lax.psum(block, axis)  207 us
    dot_general x1, matrix products, on_device(): lax.dot_general(row_flat, col_flat, (((0,), (0,)), ((), ())), precision=l...  82.4 us
    all_gather x1, waiting for transfers between devices, on_device(): raw_cols = lax.all_gather(columns, 'arc', axis=0, tiled=True)  69.9 us
    all_to_all x1, blocking collectives, measure_bands(): lax.all_to_all(jnp.stack(jnp.split(page, lax.psum(1, 'par'), axis=where_d...  43.1 us
    all_gather x1, waiting for transfers between devices, on_device(): all_mixing = lax.all_gather(mixing, 'arc', axis=0, tiled=True)  19.9 us
    dot_general x1, matrix products, on_device(): jnp.einsum('acij,acjk->acik', all_mixing, raw_cols.astype(jnp.float32), p...  18 us
  transfers between devices with their start and end apart: 3, of which 3 were waited for; matrix products, arithmetic and copies ran while one was open for 6% of the time, Pallas kernels for 0%

profile of v1, /device:TPU:0, one launch (start us, length us, event | category | flops | bytes accessed | tf_op | source)
XLA Modules:
  0.0 474.0 jit_solution(11208053893769226909)
XLA Ops:
  6.5 0.0 copy-start
  6.5 0.0 all-gather.4.cloned.1.call-start
  6.5 1.5 slice_bitcast_fusion.3
  8.0 0.0 copy-start.3
  8.1 0.2 pad_maximum_fusion
  8.3 43.1 %all_to_all.5 = bf16[4,1,3,32,2048]{4,3,2,1,0:T(8,128)(2,1)S(1)} all-to-all(bf16[4,1,3,32,2048]{4,3,2,1,0:T(8,128)(2,1)S(1)} %pad_maximum_fusion), channel_id=1, replica_groups=mesh['arc'=8,'par'=4] {'par'}, dimensions={0} | all-to-all | bytes 3145728 | tf_op jit(solution)/shard_map/all_to_all | solution.py:13
  51.4 1.2 copy.5
  52.6 0.0 all-gather.4.cloned.1.call-update
  52.6 0.0 all-gather.6.cloned.1.call-start
  52.7 0.0 copy-done.3
  52.7 0.0 copy-done
  52.7 0.4 fusion
  53.1 0.8 copy.4
  54.0 0.0 all-gather.6.cloned.1.call-update
  54.0 0.0 all-reduce.2.cloned.1.call-start
  54.1 69.9 %all-gather.4.cloned.1.call-done = bf16[8,3,128,2048]{3,2,1,0:T(8,128)(2,1)} async-done(((bf16[1,3,128,2048]{3,2,1,0:T(8,128)(2,1)}), bf16[8,3,128,2048]{3,2,1,0:T(8,128)(2,1)}) %all-gather.4.cloned.1.call-update) | async-done | bytes 12582928 | tf_op jit(solution)/shard_map/all_gather | solution.py:55
  123.9 7.5 %dynamic-slice_select_fusion = bf16[8,3,128,1024]{3,2,1,0:T(8,128)(2,1)} fusion(bf16[8,3,128,2048]{3,2,1,0:T(8,128)(2,1)} %all-gather.4.cloned.1.call-done, s32[]{:T(128)S(6)} %select_n.18, pred[]{:T(512)S(6)} %eq.22), kind=kLoop, calls=%fused_computation | loop fusion | flops 3145728 | bytes 12582917 | tf_op jit(solution)/shard_map/jit(_where)/select_n | solution.py:24
  131.5 0.0 all-reduce.2.cloned.1.call-update
  131.5 19.9 %all-gather.6.cloned.1.call-done = f32[24,128,128]{2,1,0:T(8,128)} async-done(((f32[3,128,128]{2,1,0:T(8,128)}), f32[24,128,128]{2,1,0:T(8,128)}) %all-gather.6.cloned.1.call-update) | async-done | bytes 1572880 | tf_op jit(solution)/shard_map/all_gather | solution.py:56
  151.4 0.0 copy-start.2
  151.4 18.0 %fusion.17 = f32[8,3,128,2048]{3,2,1,0:T(8,128)} fusion(f32[8,3,128,128]{3,2,1,0:T(8,128)} %bitcast.34, bf16[8,3,128,2048]{3,2,1,0:T(8,128)(2,1)} %all-gather.4.cloned.1.call-done), kind=kOutput, calls=%fused_computation.27 | convolution fusion | flops 9663676416 | bytes 39321600 | tf_op jit(solution)/shard_map/acij,acjk->acik/dot_general | solution.py:57
  169.4 207.3 %all-reduce.2.cloned.1.call-done = bf16[8,3,128,1024]{3,2,1,0:T(8,128)(2,1)} async-done(((bf16[8,3,128,1024]{3,2,1,0:T(8,128)(2,1)}), bf16[8,3,128,1024]{3,2,1,0:T(8,128)(2,1)}) %all-reduce.2.cloned.1.call-update) | async-done | bytes 6291472 | tf_op jit(solution)/shard_map/psum | solution.py:25
  376.7 0.0 copy-done.2
  376.7 8.3 %fusion.16 = f32[8,3,128,1024]{2,3,1,0:T(8,128)S(1)} fusion(f32[8,3,128,128]{3,2,1,0:T(8,128)S(1)} %bitcast.35, bf16[8,3,128,1024]{3,2,1,0:T(8,128)(2,1)} %all-reduce.2.cloned.1.call-done), kind=kOutput, calls=%fused_computation.26 | convolution fusion | flops 4831838208 | bytes 20447232 | tf_op jit(solution)/shard_map/acij,acjk->acik/dot_general | solution.py:62
  385.0 0.0 copy-start.1
  385.1 82.4 %convolution_bitcast_fusion = f32[1024,2048]{1,0:T(8,128)} fusion(f32[8,3,128,1024]{2,3,1,0:T(8,128)S(1)} %fusion.16, f32[8,3,128,2048]{3,2,1,0:T(8,128)} %fusion.17), kind=kOutput, calls=%fused_computation.1 | convolution fusion | flops 77309411328 | bytes 46137344 | tf_op jit(solution)/shard_map/dot_general | solution.py:67
  467.4 0.0 copy-done.1
  (1 shorter events, 0.0 us)
Async XLA Ops:
  6.5 46.2 %copy-start = (f32[1,3,128,128]{3,2,1,0:T(8,128)S(1)}, f32[1,3,128,128]{3,2,1,0:T(8,128)}, u32[]{:S(2)}) copy-start(f32[1,3,128,128]{3,2,1,0:T(8,128)} %param.5) | copy-start | bytes 589828
  6.5 117.4 %all-gather.4.cloned.1.call-start = ((), (), s32[]{:S(2)}) async-start(), calls=%async_computation.1 | async-start | bytes 14155776 | tf_op jit(solution)/shard_map/all_gather | solution.py:55
  8.0 44.6 %copy-start.3 = (s32[1,128]{1,0:T(1,128)S(1)}, s32[1,128]{1,0:T(1,128)}, u32[]{:S(2)}) copy-start(s32[1,128]{1,0:T(1,128)} %param.4) | copy-start | bytes 1540
  52.6 98.8 %all-gather.6.cloned.1.call-start = ((), (), s32[]{:S(2)}) async-start(), calls=%async_computation.3 | async-start | bytes 1769472 | tf_op jit(solution)/shard_map/all_gather | solution.py:56
  54.0 322.7 %all-reduce.2.cloned.1.call-start = ((), (), s32[]{:S(2)}) async-start(), calls=%async_computation.2 | async-start | bytes 12582912 | tf_op jit(solution)/shard_map/psum | solution.py:25
  151.4 225.3 %copy-start.2 = (f32[24,128,128]{2,1,0:T(8,128)S(1)}, f32[24,128,128]{2,1,0:T(8,128)}, u32[]{:S(2)}) copy-start(f32[24,128,128]{2,1,0:T(8,128)} %all-gather.6.cloned.1.call-done) | copy-start | bytes 4718596
  385.0 82.4 %copy-start.1 = (f32[1,3,128,128]{3,2,1,0:T(8,128)S(1)}, f32[1,3,128,128]{3,2,1,0:T(8,128)}, u32[]{:S(2)}) copy-start(f32[1,3,128,128]{3,2,1,0:T(8,128)} %param.5) | copy-start | bytes 589828
Sparse Core Ops, SparseCore 0:
  52.8 71.1 all-gather.3
  125.8 25.5 all-gather.5
  153.8 222.8 all-reduce.1
